TPU v7x, 512 devices: a whole 4x4x16 slice. The times are simulated.
512 devices in a mesh: frames: 32 (over z, core), phon: 4 (over y), chap: 4 (over x).
Axes of the slice: x: 4, y: 4, z: 16, core: 2. Of those that a mesh axis runs over, the one named last changes fastest.
Arguments:
- queries: bfloat16 [65536, 512], P(('chap', 'frames')), parts along dimension 0, may hold values from -80 to 80
- keys: bfloat16 [16384, 512], P(('chap', 'phon', 'frames')), parts along dimension 0, may hold values from -7 to 7
- values: bfloat16 [16384, 512], P(('chap', 'phon', 'frames')), parts along dimension 0, may hold values from -6 to 6
- band_first: int32 [128], P(('chap', 'frames')), parts along dimension 0, may hold values from 0 to 6, as said below
- cotangent: bfloat16 [65536, 512], P(('chap', 'frames')), parts along dimension 0, may hold values from -6 to 6
Outputs:
- aligned: bfloat16 [65536, 512], P(('chap', 'frames')), parts along dimension 0
- grad_query: bfloat16 [65536, 512], P(('chap', 'frames')), parts along dimension 0
- grad_key: float32 [16384, 512], P(('chap', 'phon', 'frames')), parts along dimension 0
- grad_value: float32 [16384, 512], P(('chap', 'phon', 'frames')), parts along dimension 0
There are 4 independent parts, one for each index of `chap`. A program takes and returns all parts, laid end to end along the dimension named above; each array names one. Nothing has to cross between parts.
Inputs may be any that keep to these rules, and one draw needn't show every extreme that they name: Query tile i attends the key tiles band_first[i] to band_first[i] + 1.
All inputs are finite; a program needn't handle non-finite values.
Results may differ from a plain program's by a relative error of at most 0.022.
Values may be sent and summed in bfloat16 or wider, within the bound.
No kernel may reach another device: no remote copies, remote signals or barrier semaphores. Data moves between devices by JAX's collectives and lax.ppermute only.
A program may use at most 64 MiB of HBM per device.

v0:
```python
import jax
import jax.numpy as jnp
from jax import lax
from jax.sharding import PartitionSpec as P

TILE = 512
NBAND = 2
NEG_FILL = -1e30


def in_one_piece(arrays, axis, dim, along):
    both = jnp.concatenate(arrays, axis=along)
    result, at, finished = (lax.all_gather(both, axis, axis=dim, tiled=True), 0, [])
    for a in arrays:
        finished.append(lax.slice_in_dim(result, at, at + a.shape[along], axis=along))
        at += a.shape[along]
    return tuple(finished)


def sent_to_all(value, axis):
    length = lax.axis_size(axis)
    return lax.all_to_all(
        jnp.broadcast_to(value[None], (length, *value.shape)), axis, 0, 0, tiled=True
    )


def of_everyone(value, axis):
    return sent_to_all(value, axis).max(axis=0)


def together(arrays, axis):
    ends = [0]
    for a in arrays:
        ends.append(ends[-1] + a.size)
    total = lax.psum(jnp.concatenate([a.ravel() for a in arrays]), axis)
    return tuple((total[b:e].reshape(a.shape) for a, b, e in zip(arrays, ends, ends[1:])))


def over_copies(value, axis):
    everything = sent_to_all(value, axis)
    return jnp.sum(everything.astype(jnp.float32), axis=0)


def side_by_side(arrays, axis, dim, along):
    ends, at = ([], 0)
    for a in arrays[:-1]:
        at += a.shape[along]
        ends.append(at)
    both = jnp.concatenate(arrays, axis=along)
    return tuple(
        jnp.split(lax.psum_scatter(both, axis, scatter_dimension=dim, tiled=True), ends, axis=along)
    )


def body(queries, keys, values, band_first, cotangent):
    width = queries.shape[1]
    scale = width ** (-0.5)
    block_keys, block_values = in_one_piece((keys, values), "frames", 0, 1)
    block = block_keys.shape[0]
    first_tile = lax.axis_index("phon") * (block // TILE)
    key_tile = first_tile + jnp.arange(block, dtype=jnp.int32) // TILE
    row_first = jnp.repeat(band_first, TILE)
    allowed = (key_tile[None, :] >= row_first[:, None]) & (
        key_tile[None, :] < row_first[:, None] + NBAND
    )
    key_float = block_keys.astype(jnp.float32)
    key_sq = jnp.sum(key_float * key_float, axis=1)
    raw = (
        jnp.dot(queries, block_keys.T, preferred_element_type=jnp.float32) - 0.5 * key_sq[None, :]
    ) * scale
    scores = jnp.where(allowed, raw, NEG_FILL)
    local_max = jnp.max(scores, axis=1)
    row_max = of_everyone(local_max, "phon")
    expd = jnp.where(allowed, jnp.exp(scores - row_max[:, None]), 0.0)
    part_total = jnp.sum(expd, axis=1)
    part_out = jnp.dot(expd.astype(jnp.bfloat16), block_values, preferred_element_type=jnp.float32)
    total, summed = together((part_total, part_out), "phon")
    aligned_f = summed / total[:, None]
    lse = row_max + jnp.log(total)
    back_keys, back_values = (block_keys, block_values)
    probs = jnp.where(allowed, jnp.exp(scores - lse[:, None]), 0.0)
    d_probs = jnp.dot(cotangent, back_values.T, preferred_element_type=jnp.float32)
    delta = jnp.sum(cotangent.astype(jnp.float32) * aligned_f, axis=1)
    d_scores = probs * (d_probs - delta[:, None])
    ds_low = d_scores.astype(jnp.bfloat16)
    part_query = jnp.dot(ds_low, back_keys, preferred_element_type=jnp.float32) * scale
    grad_query = (
        over_copies(part_query.astype(jnp.bfloat16), "phon")
        .astype(jnp.float32)
        .astype(jnp.bfloat16)
    )
    column_sum = jnp.sum(d_scores, axis=0)
    part_key = (
        jnp.einsum("qk,qd->kd", ds_low, queries, preferred_element_type=jnp.float32)
        - column_sum[:, None] * back_keys.astype(jnp.float32)
    ) * scale
    part_value = jnp.einsum(
        "qk,qd->kd", probs.astype(jnp.bfloat16), cotangent, preferred_element_type=jnp.float32
    )
    grad_key, grad_value = tuple(
        (
            part.astype(jnp.float32)
            for part in side_by_side(
                (part_key.astype(jnp.bfloat16), part_value.astype(jnp.bfloat16)), "frames", 0, 1
            )
        )
    )
    return (aligned_f.astype(jnp.bfloat16), grad_query, grad_key, grad_value)


def solution(mesh):
    in_specs = (
        P(("chap", "frames"), None),
        P(("chap", "phon", "frames"), None),
        P(("chap", "phon", "frames"), None),
        P(("chap", "frames")),
        P(("chap", "frames"), None),
    )
    out_specs = (
        P(("chap", "frames"), None),
        P(("chap", "frames"), None),
        P(("chap", "phon", "frames"), None),
        P(("chap", "phon", "frames"), None),
    )
    return jax.shard_map(body, mesh=mesh, in_specs=in_specs, out_specs=out_specs, check_vma=False)
```

profile of v0, /device:TPU:28, one launch (start us, length us, event | category | flops | bytes accessed | tf_op | source)
XLA Modules:
  0.0 291.1 jit_solution(5057413454272372290)
XLA Ops:
  7.2 0.0 copy-start
  7.2 0.0 all-gather.2.cloned.1.call-start
  7.2 1.5 pad_maximum_fusion.2
  8.7 0.0 all-gather.2.cloned.1.call-update
  8.7 0.0 all-reduce.2.cloned.1.call-start
  9.4 76.9 %all-gather.2.cloned.1.call-done = bf16[1024,1024]{1,0:T(8,128)(2,1)} async-done(((bf16[32,1024]{1,0:T(8,128)(2,1)}), bf16[1024,1024]{1,0:T(8,128)(2,1)}) %all-gather.2.cloned.1.call-update) | async-done | bytes 2097168 | tf_op jit(solution)/shard_map/all_gather | solution.py:13
  86.3 1.5 fusion
  87.8 0.0 copy-done
  87.8 2.0 fusion.32
  89.8 0.0 copy-start.1
  89.9 7.8 %all_to_all.11 = f32[4,1,512]{2,1,0:T(1,128)S(1)} all-to-all(f32[4,1,512]{2,1,0:T(1,128)S(1)} %broadcast_in_dim.13), channel_id=1, replica_groups=mesh['frames'=32,'phon'=4,'chap'=4] {'phon'}, dimensions={0} | all-to-all | bytes 16384 | tf_op jit(solution)/shard_map/all_to_all | solution.py:22
  97.7 0.0 copy-start.3
  97.7 0.4 fusion.4
  98.1 1.2 copy-done.3
  99.3 0.9 convolution_bitcast_fusion
  100.2 0.0 copy-done.1
  100.2 0.3 copy.23
  100.5 1.1 pad_maximum_fusion.1
  101.6 0.0 all-reduce.2.cloned.1.call-update
  101.6 0.0 copy-start.6
  101.6 0.0 reduce-scatter.2.cloned.1.call-start
  101.7 57.8 %all-reduce.2.cloned.1.call-done = f32[262656]{0:T(1024)} async-done(((f32[262656]{0:T(1024)}), f32[262656]{0:T(1024)}) %all-reduce.2.cloned.1.call-update) | async-done | bytes 1050640 | tf_op jit(solution)/shard_map/psum | solution.py:35
  159.5 1.3 slice.29
  160.8 0.2 slice.25
  160.9 0.7 log_add_fusion
  161.6 0.0 copy-done.6
  161.6 0.0 copy-start.4
  161.6 2.5 convolution_convert_fusion
  164.1 0.0 copy-start.2
  164.1 1.0 multiply_reduce_fusion
  165.2 0.0 copy-done.4
  165.2 0.7 copy-done.2
  165.9 1.1 fusion.33
  167.0 0.0 copy-start.7
  167.0 0.7 fusion.3
  167.7 0.2 copy-done.7
  167.9 1.6 pad_maximum_fusion
  169.5 0.0 copy-start.5
  169.5 0.0 reduce-scatter.2.cloned.1.call-update
  169.5 1.6 copy-done.5
  171.1 2.0 fusion.7
  173.0 0.2 broadcast_in_dim.15
  173.2 27.1 %all_to_all.12 = bf16[4,512,512]{2,1,0:T(8,128)(2,1)S(1)} all-to-all(bf16[4,512,512]{2,1,0:T(8,128)(2,1)S(1)} %broadcast_in_dim.15), channel_id=1, replica_groups=mesh['frames'=32,'phon'=4,'chap'=4] {'phon'}, dimensions={0} | all-to-all | bytes 4194304 | tf_op jit(solution)/shard_map/all_to_all | solution.py:22
  200.3 1.2 reduce_sum.51
  201.5 81.6 %reduce-scatter.2.cloned.1.call-done = bf16[32,1024]{1,0:T(8,128)(2,1)} async-done(((bf16[1024,1024]{1,0:T(8,128)(2,1)}), bf16[32,1024]{1,0:T(8,128)(2,1)}) %reduce-scatter.2.cloned.1.call-update) | async-done | bytes 65552 | tf_op jit(solution)/shard_map/reduce_scatter | solution.py:51
  283.2 1.4 slice_convert_fusion
  (4 shorter events, 0.0 us)
Async XLA Ops:
  7.2 80.7 %copy-start = (bf16[512,512]{1,0:T(8,128)(2,1)S(1)}, bf16[512,512]{1,0:T(8,128)(2,1)}, u32[]{:S(2)}) copy-start(bf16[512,512]{1,0:T(8,128)(2,1)} %param.5) | copy-start | bytes 1572868
  7.2 79.1 %all-gather.2.cloned.1.call-start = ((), (), s32[]{:S(2)}) async-start(), calls=%async_computation.3 | async-start | bytes 2162688 | tf_op jit(solution)/shard_map/all_gather | solution.py:13
  8.7 150.7 %all-reduce.2.cloned.1.call-start = ((), (), s32[]{:S(2)}) async-start(), calls=%async_computation.4 | async-start | bytes 2105344 | tf_op jit(solution)/shard_map/psum | solution.py:35
  89.8 10.4 %copy-start.1 = (f32[1024,512]{1,0:T(8,128)}, f32[1024,512]{1,0:T(8,128)S(1)}, u32[]{:S(2)}) copy-start(f32[1024,512]{1,0:T(8,128)S(1)} %get-tuple-element.11) | copy-start | bytes 6291460
  97.7 1.6 copy-start.3
  101.6 60.0 %copy-start.6 = (bf16[512,512]{1,0:T(8,128)(2,1)S(1)}, bf16[512,512]{1,0:T(8,128)(2,1)}, u32[]{:S(2)}) copy-start(bf16[512,512]{1,0:T(8,128)(2,1)} %param.9) | copy-start | bytes 1572868
  101.6 181.5 %reduce-scatter.2.cloned.1.call-start = ((), (), s32[]{:S(2)}) async-start(), calls=%async_computation.5 | async-start | bytes 2162688 | tf_op jit(solution)/shard_map/reduce_scatter | solution.py:51
  161.6 3.5 %copy-start.4 = (bf16[1024,1024]{1,0:T(8,128)(2,1)S(1)}, bf16[1024,1024]{1,0:T(8,128)(2,1)}, u32[]{:S(2)}) copy-start(bf16[1024,1024]{1,0:T(8,128)(2,1)} %all-gather.2.cloned.1.call-done) | copy-start | bytes 6291460
  164.1 1.8 copy-start.2
  167.0 1.0 copy-start.7
  169.5 1.6 copy-start.5
Sparse Core Ops, SparseCore 0:
  10.7 75.5 all-gather.1
  101.7 57.6 all-reduce.1
  169.6 113.4 reduce-scatter.1
where the time goes:
time: 292 us; the launch traced here: 291 us
  waiting for transfers between devices  216 us (74%)
  blocking collectives  34.9 us (12%)
  between operations  14.5 us (5%)
  other arithmetic  10.4 us (4%)
  matrix products  9.13 us (3%)
  local copies, waits for them, and re-layouts  5.67 us (2%)
    reduce_scatter x1, waiting for transfers between devices, side_by_side(): lax.psum_scatter(both, axis, scatter_dimension=dim, tiled=True)  81.6 us
    all_gather x1, waiting for transfers between devices, in_one_piece(): lax.all_gather(both, axis, axis=dim, tiled=True)  76.9 us
    psum x1, waiting for transfers between devices, together(): total = lax.psum(jnp.concatenate([a.ravel() for a in arrays]), axis)  57.8 us
    all_to_all x2, blocking collectives, sent_to_all(): lax.all_to_all(jnp.broadcast_to(value[None], (length, *value.shape)), axi...  34.9 us
  transfers between devices with their start and end apart: 3, of which 3 were waited for; matrix products, arithmetic and copies ran while one was open for 1% of the time, Pallas kernels for 0%

commit v1 on v0

--- a/solution.py
+++ b/solution.py
@@ -32,7 +32,7 @@
     ends = [0]
     for a in arrays:
         ends.append(ends[-1] + a.size)
-    total = lax.psum(jnp.concatenate([a.ravel() for a in arrays]), axis)
+    total = jnp.sum(lax.all_gather(jnp.concatenate([a.ravel() for a in arrays]), axis), axis=0)
     return tuple((total[b:e].reshape(a.shape) for a, b, e in zip(arrays, ends, ends[1:])))
 
 

time: 292 us -> 310 us (1.062)
  the two profiles are of different devices: /device:TPU:28 before, /device:TPU:24 now
where the time goes in v1:
time: 310 us; the launch traced here: 309 us
  waiting for transfers between devices  208 us (67%)
  blocking collectives  37.4 us (12%)
  other arithmetic  29.3 us (9%)
  between operations  14.6 us (5%)
  local copies, waits for them, and re-layouts  10.9 us (4%)
  matrix products  9.12 us (3%)
    reduce_scatter x1, waiting for transfers between devices, side_by_side(): lax.psum_scatter(both, axis, scatter_dimension=dim, tiled=True)  80 us
    all_gather x1, waiting for transfers between devices, in_one_piece(): lax.all_gather(both, axis, axis=dim, tiled=True)  76.9 us
    all_gather x1, waiting for transfers between devices, together(): lax.all_gather(jnp.concatenate([a.ravel() for a in arrays]), axis)  51 us
    all_to_all x2, blocking collectives, sent_to_all(): lax.all_to_all(jnp.broadcast_to(value[None], (length, *value.shape)), axi...  37.4 us
    reduce_sum x1, other arithmetic, together(): jnp.sum(lax.all_gather(jnp.concatenate([a.ravel() for a in arrays]), axis...  20.5 us
    unnamed x18, local copies, waits for them, and re-layouts  10.5 us
  transfers between devices with their start and end apart: 3, of which 3 were waited for; matrix products, arithmetic and copies ran while one was open for 1% of the time, Pallas kernels for 0%

profile of v1, /device:TPU:24, one launch (start us, length us, event | category | flops | bytes accessed | tf_op | source)
XLA Modules:
  0.0 309.4 jit_solution(17585557859611757439)
XLA Ops:
  7.2 0.0 copy-start
  7.2 0.0 all-gather.5.cloned.1.call-start
  7.2 1.5 pad_maximum_fusion.2
  8.7 0.0 all-gather.5.cloned.1.call-update
  8.7 0.0 all-gather.7.cloned.1.call-start
  9.4 76.9 %all-gather.5.cloned.1.call-done = bf16[1024,1024]{1,0:T(8,128)(2,1)} async-done(((bf16[32,1024]{1,0:T(8,128)(2,1)}), bf16[1024,1024]{1,0:T(8,128)(2,1)}) %all-gather.5.cloned.1.call-update) | async-done | bytes 2097168 | tf_op jit(solution)/shard_map/all_gather | solution.py:13
  86.4 1.5 fusion
  87.9 0.0 copy-done
  87.9 2.0 fusion.32
  89.9 0.0 copy-start.1
  89.9 7.8 %all_to_all.11 = f32[4,1,512]{2,1,0:T(1,128)S(1)} all-to-all(f32[4,1,512]{2,1,0:T(1,128)S(1)} %broadcast_in_dim.13), channel_id=1, replica_groups=mesh['frames'=32,'phon'=4,'chap'=4] {'phon'}, dimensions={0} | all-to-all | bytes 16384 | tf_op jit(solution)/shard_map/all_to_all | solution.py:22
  97.8 0.0 copy-start.3
  97.8 0.4 fusion.4
  98.2 1.2 copy-done.3
  99.4 0.9 convolution_bitcast_fusion
  100.3 0.0 copy-done.1
  100.3 0.3 copy.26
  100.5 0.1 pad_maximum_fusion.1
  100.6 5.7 %reshape.53 = f32[1,1,262656]{2,1,0:T(1,128)} reshape(f32[262656]{0:T(1024)S(1)} %pad_maximum_fusion.1) | data formatting | bytes 2101248
  106.3 0.0 all-gather.7.cloned.1.call-update
  106.3 0.0 reduce-scatter.2.cloned.1.call-start
  106.4 51.0 %all-gather.7.cloned.1.call-done = f32[4,1,262656]{2,1,0:T(1,128)} async-done(((f32[1,1,262656]{2,1,0:T(1,128)}), f32[4,1,262656]{2,1,0:T(1,128)}) %all-gather.7.cloned.1.call-update) | async-done | bytes 4202512 | tf_op jit(solution)/shard_map/all_gather | solution.py:35
  157.3 20.5 %reduce_sum.59 = f32[262656]{0:T(1024)S(1)} reduce(f32[4,1,262656]{2,1,0:T(1,128)} %all-gather.7.cloned.1.call-done, f32[]{:T(128)} %constant.34.clone.1), dimensions={0,1}, to_apply=%region_4.5 | reduce | flops 787968 | bytes 5253124 | tf_op jit(solution)/shard_map/reduce_sum | solution.py:35
  177.9 0.0 copy-start.6
  177.9 0.1 slice.29
  178.0 0.2 slice.25
  178.2 0.8 copy-done.6
  178.9 0.0 copy-start.4
  178.9 2.5 convolution_convert_fusion
  181.4 0.0 copy-start.2
  181.5 1.0 multiply_reduce_fusion
  182.5 0.0 copy-done.4
  182.5 0.7 copy-done.2
  183.2 1.1 fusion.33
  184.3 0.0 copy-start.7
  184.3 0.7 fusion.3
  185.0 0.3 copy-done.7
  185.3 1.6 pad_maximum_fusion
  186.9 0.0 copy-start.5
  186.9 0.0 reduce-scatter.2.cloned.1.call-update
  186.9 1.6 copy-done.5
  188.5 2.0 fusion.7
  190.4 0.2 broadcast_in_dim.15
  190.6 29.6 %all_to_all.12 = bf16[4,512,512]{2,1,0:T(8,128)(2,1)S(1)} all-to-all(bf16[4,512,512]{2,1,0:T(8,128)(2,1)S(1)} %broadcast_in_dim.15), channel_id=1, replica_groups=mesh['frames'=32,'phon'=4,'chap'=4] {'phon'}, dimensions={0} | all-to-all | bytes 4194304 | tf_op jit(solution)/shard_map/all_to_all | solution.py:22
  220.2 1.2 reduce_sum.61
  221.4 80.0 %reduce-scatter.2.cloned.1.call-done = bf16[32,1024]{1,0:T(8,128)(2,1)} async-done(((bf16[1024,1024]{1,0:T(8,128)(2,1)}), bf16[32,1024]{1,0:T(8,128)(2,1)}) %reduce-scatter.2.cloned.1.call-update) | async-done | bytes 65552 | tf_op jit(solution)/shard_map/reduce_scatter | solution.py:51
  301.4 1.4 slice_convert_fusion
  (5 shorter events, 0.0 us)
Async XLA Ops:
  7.2 80.7 %copy-start = (bf16[512,512]{1,0:T(8,128)(2,1)S(1)}, bf16[512,512]{1,0:T(8,128)(2,1)}, u32[]{:S(2)}) copy-start(bf16[512,512]{1,0:T(8,128)(2,1)} %param.5) | copy-start | bytes 1572868
  7.2 79.2 %all-gather.5.cloned.1.call-start = ((), (), s32[]{:S(2)}) async-start(), calls=%async_computation.3 | async-start | bytes 2162688 | tf_op jit(solution)/shard_map/all_gather | solution.py:13
  8.7 148.6 %all-gather.7.cloned.1.call-start = ((), (), s32[]{:S(2)}) async-start(), calls=%async_computation.5 | async-start | bytes 5253120 | tf_op jit(solution)/shard_map/all_gather | solution.py:35
  89.9 10.4 %copy-start.1 = (f32[1024,512]{1,0:T(8,128)}, f32[1024,512]{1,0:T(8,128)S(1)}, u32[]{:S(2)}) copy-start(f32[1024,512]{1,0:T(8,128)S(1)} %get-tuple-element.11) | copy-start | bytes 6291460
  97.8 1.6 copy-start.3
  106.3 195.1 %reduce-scatter.2.cloned.1.call-start = ((), (), s32[]{:S(2)}) async-start(), calls=%async_computation.4 | async-start | bytes 2162688 | tf_op jit(solution)/shard_map/reduce_scatter | solution.py:51
  177.9 1.0 copy-start.6
  178.9 3.5 %copy-start.4 = (bf16[1024,1024]{1,0:T(8,128)(2,1)S(1)}, bf16[1024,1024]{1,0:T(8,128)(2,1)}, u32[]{:S(2)}) copy-start(bf16[1024,1024]{1,0:T(8,128)(2,1)} %all-gather.5.cloned.1.call-done) | copy-start | bytes 6291460
  181.4 1.8 copy-start.2
  184.3 1.0 copy-start.7
  186.9 1.6 copy-start.5
Sparse Core Ops, SparseCore 0:
  10.7 75.6 all-gather.4
  106.4 50.8 all-gather.6
  187.0 114.3 reduce-scatter.1
